TPU v7x, 32 devices: a whole 2x2x4 slice. The times are simulated.
32 devices in a mesh: groups: 2 (over x), dev: 8 (over z, y), sub: 2 (over core).
Axes of the slice: x: 2, y: 2, z: 4, core: 2. Of those that a mesh axis runs over, the one named last changes fastest.
Arguments:
- hidden: bfloat16 [1024, 2048], P(('groups', 'dev', 'sub')), parts along dimension 0, may hold values from -6 to 6
- lengths: int32 [32, 32], P(('groups', 'dev', 'sub')), parts along dimension 0, may hold values from 1 to 256, 4096 in all within a row
- key_cache: bfloat16 [32, 4096, 512], P(('groups', 'dev', 'sub')), parts along dimension 0, may hold values from -320 to 320
- value_cache: bfloat16 [32, 4096, 512], P(('groups', 'dev', 'sub')), parts along dimension 0, may hold values from -6 to 6
- expert_ids: int32 [1024, 8], P(('groups', 'dev', 'sub')), parts along dimension 0, may hold values from 0 to 15, all different within a row; in each aligned block of 32 rows (0 to 31, 32 to 63, ...) at most 16 rows name the same one
- gate_codes: int32 [1024, 8], P(('groups', 'dev', 'sub')), parts along dimension 0, may hold values from 1 to 1023
- expert_device: int32 [16], replicated, may hold values from 0 to 15, each once
- attention_gain: float32 [2048], replicated, may hold values from 0.1 to 1.9
- mixture_gain: float32 [2048], replicated, may hold values from 0.1 to 1.9
- query_gain: float32 [128], replicated, may hold values from 0.1 to 1.9
- key_gain: float32 [128], replicated, may hold values from 0.1 to 1.9
- project_weight: bfloat16 [2048, 5120], P(None, 'dev'), may hold values from -0.125 to 0.125
- output_weight: bfloat16 [4096, 2048], P('dev'), may hold values from -0.09375 to 0.09375
- expert_gate_up: bfloat16 [16, 2048, 1536], P(('dev', 'sub')), may hold values from -0.125 to 0.125
- expert_down: bfloat16 [16, 768, 2048], P(('dev', 'sub')), may hold values from -0.21875 to 0.21875
Outputs:
- layer_out: bfloat16 [1024, 2048], P(('groups', 'dev', 'sub')), parts along dimension 0
There are 2 independent parts, one for each index of `groups`. A program takes and returns all parts, laid end to end along the dimension named above; an argument that names none is the same for every part. Nothing has to cross between parts.
Inputs may be any that keep to these rules, and one draw needn't show every extreme that they name: `expert_ids`: each row names 8 different experts. Among the 32 rows of one device no expert is named more than 16 times, and in some device an expert is named exactly 16 times. The 32 lengths of each device sum to 4096; the largest of them is 256. A permutation: expert e is held by the device at index expert_device[e] of the joined axes dev and sub.
All inputs are finite; a program needn't handle non-finite values.
Results may differ from a plain program's by a relative error of at most 0.015.
Values may be sent and summed in bfloat16 or wider, within the bound.
A program may use at most 128 MiB of HBM per device.

v0:
```python
import math

import jax
import jax.numpy as jnp
from jax import lax
from jax.sharding import PartitionSpec as P

D = 2048
HEADS = 32
KVH = 4
HD = 128
TOP = 8
CAP = 16


EPSILON = 1e-06
ROPE_BASE = 1000000.0


def norm_scale(values, scale_gain):
    mean_square = jnp.mean(values * values, axis=-1, keepdims=True)
    return values * lax.rsqrt(mean_square + EPSILON) * scale_gain


def rotate(values, position):
    half_width = values.shape[-1] // 2
    frequency = ROPE_BASE ** (-jnp.arange(half_width, dtype=jnp.float32) * 2.0 / values.shape[-1])
    angles = position.astype(jnp.float32)[:, None] * frequency[None, :]
    cosine = jnp.cos(angles)[:, None, :]
    sine_part = jnp.sin(angles)[:, None, :]
    first_half = values[..., :half_width]
    second_half = values[..., half_width:]
    return jnp.concatenate(
        [
            first_half * cosine - second_half * sine_part,
            second_half * cosine + first_half * sine_part,
        ],
        axis=-1,
    )


def split_heads(merged, position, query_gain, key_gain):
    row_count = merged.shape[0]
    query_cols = HEADS * HD
    key_cols = KVH * HD
    queries = merged[:, :query_cols].astype(jnp.float32).reshape(row_count, HEADS, HD)
    queries = rotate(norm_scale(queries, query_gain), position).astype(jnp.bfloat16)
    new_keys = (
        merged[:, query_cols : query_cols + key_cols]
        .astype(jnp.float32)
        .reshape(row_count, KVH, HD)
    )
    new_keys = rotate(norm_scale(new_keys, key_gain), position).astype(jnp.bfloat16)
    new_values = merged[:, query_cols + key_cols :].reshape(row_count, KVH, HD)
    return (queries, new_keys, new_values)


def attend(queries, new_keys, new_values, key_rows, value_rows, lengths):
    row_count, head_count, head_width = queries.shape
    kv_count = new_keys.shape[1]
    group_size = head_count // kv_count
    pool_size = key_rows.shape[0]
    seg_end = jnp.cumsum(lengths)
    seg_start = seg_end - lengths
    position = jnp.arange(pool_size, dtype=jnp.int32)
    inside = (position[None, :] >= seg_start[:, None]) & (position[None, :] < seg_end[:, None])
    grouped = queries.reshape(row_count, kv_count, group_size, head_width)
    keyed = key_rows.reshape(pool_size, kv_count, head_width)
    valued = value_rows.reshape(pool_size, kv_count, head_width)
    scale = 1.0 / math.sqrt(head_width)
    scores = (
        jnp.einsum("rkgd,pkd->krgp", grouped, keyed, preferred_element_type=jnp.float32) * scale
    )
    own_score = (
        jnp.einsum("rkgd,rkd->krg", grouped.astype(jnp.float32), new_keys.astype(jnp.float32))
        * scale
    )
    mask = inside[None, :, None, :]
    masked = jnp.where(mask, scores, -1e30)
    peak = jnp.maximum(jnp.max(masked, axis=3), own_score)
    raised = jnp.where(mask, jnp.exp(masked - peak[..., None]), 0.0)
    own_raised = jnp.exp(own_score - peak)
    denominator = jnp.sum(raised, axis=3) + own_raised
    weights = (raised / denominator[..., None]).astype(jnp.bfloat16)
    mixed_out = jnp.einsum("krgp,pkd->rkgd", weights, valued, preferred_element_type=jnp.float32)
    own_weight = jnp.transpose(own_raised / denominator, (1, 0, 2))[..., None]
    own_part = own_weight * new_values.astype(jnp.float32)[:, :, None, :]
    return (mixed_out + own_part).reshape(row_count, head_count * head_width).astype(jnp.bfloat16)


def expert_block(arrived, gate_up, down_rows):
    count = arrived.shape[0] * arrived.shape[1]
    flat = arrived.reshape(count, arrived.shape[2])
    both_parts = jnp.dot(flat, gate_up, preferred_element_type=jnp.float32)
    inner = down_rows.shape[0]
    units = (jax.nn.silu(both_parts[:, :inner]) * both_parts[:, inner:]).astype(jnp.bfloat16)
    result = jnp.dot(units, down_rows, preferred_element_type=jnp.float32).astype(jnp.bfloat16)
    return result.reshape(arrived.shape)


def on_device(
    hidden,
    lengths,
    key_cache,
    value_cache,
    expert_ids,
    gate_codes,
    expert_device,
    attention_gain,
    mixture_gain,
    query_gain,
    key_gain,
    project_weight,
    output_weight,
    expert_gate_up,
    expert_down,
):
    row_count = hidden.shape[0]
    normed = norm_scale(hidden.astype(jnp.float32), attention_gain).astype(jnp.bfloat16)
    merged_cols = jnp.dot(
        lax.all_gather(normed, "dev", axis=0, tiled=True),
        project_weight,
        preferred_element_type=jnp.float32,
    ).astype(jnp.bfloat16)
    merged = lax.all_to_all(merged_cols, "dev", split_axis=0, concat_axis=1, tiled=True)
    position = lengths.reshape(row_count)
    queries, new_keys, new_values = split_heads(merged, position, query_gain, key_gain)
    attention = attend(queries, new_keys, new_values, key_cache[0], value_cache[0], position)
    features = lax.all_to_all(attention, "dev", split_axis=1, concat_axis=0, tiled=True)
    projected = lax.psum_scatter(
        jnp.dot(features, output_weight, preferred_element_type=jnp.float32).astype(jnp.bfloat16),
        "dev",
        scatter_dimension=0,
        tiled=True,
    ).astype(jnp.float32)
    residual = hidden.astype(jnp.float32) + projected
    mixture_in = norm_scale(residual, mixture_gain).astype(jnp.bfloat16)
    expert_count = expert_device.shape[0]
    expert_range = jnp.arange(expert_count, dtype=jnp.int32)
    holder = jnp.sum(
        jnp.where(
            expert_ids[:, :, None] == expert_range[None, None, :], expert_device[None, None, :], 0
        ),
        axis=2,
    )
    flat_holder = holder.reshape(row_count * TOP)
    onehot = (flat_holder[:, None] == expert_range[None, :]).astype(jnp.int32)
    before = jnp.cumsum(onehot, axis=0) - onehot
    slot_index = jnp.sum(before * onehot, axis=1)
    target = flat_holder * CAP + slot_index
    cell_index = jnp.arange(expert_count * CAP, dtype=jnp.int32)
    matched = (target[:, None] == cell_index[None, :]).reshape(row_count, TOP, expert_count * CAP)
    assign = jnp.any(matched, axis=1).astype(jnp.bfloat16)
    share = gate_codes.astype(jnp.float32)
    share = share / jnp.sum(share, axis=1, keepdims=True)
    combine = jnp.sum(jnp.where(matched, share[:, :, None], 0.0), axis=1)
    outgoing = jnp.einsum(
        "rc,rd->cd", assign, mixture_in, preferred_element_type=jnp.float32
    ).astype(jnp.bfloat16)
    outgoing = outgoing.reshape(expert_count, CAP, D)
    gate_up = expert_gate_up[0]
    down_rows = expert_down[0]
    computed = expert_block(
        lax.all_to_all(outgoing, ("dev", "sub"), split_axis=0, concat_axis=0, tiled=True),
        gate_up,
        down_rows,
    )
    returned = lax.all_to_all(computed, ("dev", "sub"), split_axis=0, concat_axis=0, tiled=True)
    returned_flat = returned.reshape(expert_count * CAP, D).astype(jnp.float32)
    routed = jnp.dot(combine, returned_flat, precision=lax.Precision.HIGHEST)
    return (residual + routed).astype(jnp.bfloat16)


def solution(mesh):
    return jax.shard_map(
        on_device,
        mesh=mesh,
        in_specs=(
            P(("groups", "dev", "sub"), None),
            P(("groups", "dev", "sub"), None),
            P(("groups", "dev", "sub"), None, None),
            P(("groups", "dev", "sub"), None, None),
            P(("groups", "dev", "sub"), None),
            P(("groups", "dev", "sub"), None),
            P(),
            P(),
            P(),
            P(),
            P(),
            P(None, "dev"),
            P("dev", None),
            P(("dev", "sub"), None, None),
            P(("dev", "sub"), None, None),
        ),
        out_specs=P(("groups", "dev", "sub"), None),
        check_vma=False,
    )
```

profile of v0, /device:TPU:0, one launch (start us, length us, event | category | flops | bytes accessed | tf_op | source)
XLA Modules:
  0.0 252.8 jit_solution(13442766343679465597)
XLA Ops:
  6.5 1.2 fusion.27
  7.7 1.7 fusion.29
  10.3 6.9 %reshape_squeeze.6 = bf16[4096,4,128]{2,1,0:T(4,128)(2,1)} reshape(bf16[1,4096,512]{2,1,0:T(8,128)(2,1)} %param.17) | data formatting | bytes 8388608 | tf_op jit(solution)/shard_map/reshape;squeeze | solution.py:68
  17.3 7.0 %reshape_squeeze.7 = bf16[4096,4,128]{2,1,0:T(4,128)(2,1)} reshape(bf16[1,4096,512]{2,1,0:T(8,128)(2,1)} %param.18) | data formatting | bytes 8388608 | tf_op jit(solution)/shard_map/reshape;squeeze | solution.py:69
  24.4 28.1 %all-gather.2.cloned.1.call-done = bf16[256,2048]{1,0:T(8,128)(2,1)} async-done(((bf16[32,2048]{1,0:T(8,128)(2,1)}), bf16[256,2048]{1,0:T(8,128)(2,1)}) %all-gather.2.cloned.1.call-update) | async-done | bytes 1048592 | tf_op jit(solution)/shard_map/all_gather | solution.py:121
  52.6 3.8 %convolution_convert_fusion.2 = bf16[256,640]{1,0:T(8,128)(2,1)} fusion(bf16[256,2048]{1,0:T(8,128)(2,1)} %all-gather.2.cloned.1.call-done, bf16[2048,640]{1,0:T(8,128)(2,1)} %param.26), kind=kOutput, calls=%fused_computation.20 | convolution fusion | flops 671252480 | bytes 3997696 | tf_op jit(solution)/shard_map/dot_general | solution.py:120
  56.4 4.1 %all-to-all-start = ((bf16[8,32,640]{2,1,0:T(8,128)(2,1)}), bf16[8,32,640]{2,1,0:T(8,128)(2,1)}, u32[]{:S(2)}, u32[]{:S(2)}) async-start(bf16[8,32,640]{2,1,0:T(8,128)(2,1)} %bitcast.2), calls=%async_computation | async-start | bytes 655360 | tf_op jit(solution)/shard_map/all_to_all | solution.py:125
  60.7 8.7 %all-to-all-done = bf16[8,32,640]{2,1,0:T(8,128)(2,1)} async-done(((bf16[8,32,640]{2,1,0:T(8,128)(2,1)}), bf16[8,32,640]{2,1,0:T(8,128)(2,1)}, u32[]{:S(2)}, u32[]{:S(2)}) %all-to-all-start) | async-done | bytes 327712 | tf_op jit(solution)/shard_map/all_to_all | solution.py:125
  71.3 1.1 copy.72
  73.9 6.5 %fusion = (f32[4,32,8]{2,1,0:T(8,128)S(1)}, f32[4,32,8,4096]{3,2,1,0:T(8,128)S(1)}) fusion(pred[32,4096]{1,0:T(8,128)(4,1)S(1)} %fusion.24, bf16[4096,4,128,1]{2,1,0,3:T(4,128)(2,1)} %bitcast.83, bf16[32,4,8,128]{3,2,1,0:T(8,128)(2,1)S(1)} %pad_maximum_fusion), kind=kOutput, calls=%fused_computation.3 | convolution fusion | flops 1086323712 | bytes 21368832 | tf_op jit(solution)/shard_map/rkgd,pkd->krgp/dot_general | solution.py:72
  80.4 6.0 %fusion.1 = f32[4,32,8]{2,1,0:T(8,128)S(1)} fusion(f32[4,32,8,4096]{3,2,1,0:T(8,128)S(1)} %get-tuple-element.14, f32[4,32,8]{2,1,0:T(8,128)S(1)} %multiply_maximum_fusion, pred[32,4096]{1,0:T(8,128)(4,1)S(1)} %fusion.24), kind=kLoop, calls=%fused_computation.4 | loop fusion | flops 20970496 | bytes 16916480 | tf_op jit(solution)/shard_map/reduce_sum | solution.py:83
  86.5 11.2 %fusion.20 = bf16[32,4,8,128]{3,2,0,1:T(8,128)(2,1)S(1)} fusion(bf16[4096,4,128,1]{2,1,0,3:T(4,128)(2,1)} %bitcast.85, f32[4,32,8,4096]{3,2,1,0:T(8,128)} %copy-done.1, f32[4,32,8]{2,1,0:T(8,128)S(1)} %exponential_add_fusion, f32[4,32,8]{2,1,0:T(8,128)S(1)} %multiply_maximum_fusion, pred[32,4096]{1,0:T(8,128)(4,1)S(1)} %fusion.24, ...), kind=kOutput, calls=%fused_computation.21 | convolution fusion | flops 1099300864 | bytes 21442560 | tf_op jit(solution)/shard_map/krgp,pkd->rkgd/dot_general | solution.py:85
  98.7 1.0 copy.53
  99.7 11.6 %all_to_all.45 = bf16[32,8,512]{2,0,1:T(8,128)(2,1)S(1)} all-to-all(bf16[32,8,512]{2,0,1:T(8,128)(2,1)S(1)} %copy.53), channel_id=1, replica_groups=mesh['groups'=2,'dev'=8,'sub'=2] {'dev'}, dimensions={1} | all-to-all | bytes 524288 | tf_op jit(solution)/shard_map/all_to_all | solution.py:129
  111.4 3.3 %convolution_convert_fusion = bf16[256,2048]{1,0:T(8,128)(2,1)} fusion(bf16[256,512]{1,0:T(8,128)(2,1)S(1)} %bitcast.91, bf16[512,2048]{1,0:T(8,128)(2,1)} %param.27), kind=kOutput, calls=%fused_computation.13 | convolution fusion | flops 537395200 | bytes 3407872 | tf_op jit(solution)/shard_map/dot_general | solution.py:131
  116.4 61.7 %reduce-scatter.2.cloned.1.call-done = bf16[32,2048]{1,0:T(8,128)(2,1)} async-done(((bf16[256,2048]{1,0:T(8,128)(2,1)}), bf16[32,2048]{1,0:T(8,128)(2,1)}) %reduce-scatter.2.cloned.1.call-update) | async-done | bytes 131088 | tf_op jit(solution)/shard_map/reduce_scatter | solution.py:130
  178.1 1.1 multiply_reduce_fusion.1
  179.2 1.4 convolution_convert_fusion.1
  180.6 28.1 %all_to_all.46 = bf16[16,16,2048]{2,1,0:T(8,128)(2,1)S(1)} all-to-all(bf16[16,16,2048]{2,1,0:T(8,128)(2,1)S(1)} %bitcast.86), channel_id=1, replica_groups=mesh['groups'=2,'dev'=8,'sub'=2] {'dev','sub'}, dimensions={0} | all-to-all | bytes 2097152 | tf_op jit(solution)/shard_map/all_to_all | solution.py:164
  208.8 4.6 %fusion.3 = f32[256,1536]{1,0:T(8,128)S(1)} fusion(bf16[256,2048]{1,0:T(8,128)(2,1)S(1)} %bitcast.90, bf16[1,2048,1536]{2,1,0:T(8,128)(2,1)} %param.28), kind=kOutput, calls=%fused_computation.6 | convolution fusion | flops 1610612736 | bytes 8912896 | tf_op jit(solution)/shard_map/dot_general | solution.py:94
  213.4 2.1 fusion.10
  215.5 5.1 %all-to-all-start.3 = ((bf16[16,16,2048]{2,1,0:T(8,128)(2,1)}), bf16[16,16,2048]{2,1,0:T(8,128)(2,1)}, u32[]{:S(2)}, u32[]{:S(2)}) async-start(bf16[16,16,2048]{2,1,0:T(8,128)(2,1)} %bitcast.89), calls=%async_computation.4 | async-start | bytes 2097152 | tf_op jit(solution)/shard_map/all_to_all | solution.py:168
  220.8 22.7 %all-to-all-done.3 = bf16[16,16,2048]{2,1,0:T(8,128)(2,1)} async-done(((bf16[16,16,2048]{2,1,0:T(8,128)(2,1)}), bf16[16,16,2048]{2,1,0:T(8,128)(2,1)}, u32[]{:S(2)}, u32[]{:S(2)}) %all-to-all-start.3) | async-done | bytes 1048608 | tf_op jit(solution)/shard_map/all_to_all | solution.py:168
  243.5 2.5 fusion.13
  (76 shorter events, 7.7 us)
Async XLA Ops:
  6.5 206.8 %copy-start = (bf16[1,768,2048]{2,1,0:T(8,128)(2,1)S(1)}, bf16[1,768,2048]{2,1,0:T(8,128)(2,1)}, u32[]{:S(2)}) copy-start(bf16[1,768,2048]{2,1,0:T(8,128)(2,1)} %param.29) | copy-start | bytes 9437188
  6.5 46.0 %all-gather.2.cloned.1.call-start = ((), (), s32[]{:S(2)}) async-start(), calls=%async_computation.5 | async-start | bytes 1179648 | tf_op jit(solution)/shard_map/all_gather | solution.py:121
  17.3 7.0 %copy-start.9 = (s32[1,32]{1,0:T(1,128)S(1)}, s32[1,32]{1,0:T(1,128)}, u32[]{:S(2)}) copy-start(s32[1,32]{1,0:T(1,128)} %param.16) | copy-start | bytes 388
  24.2 48.5 %copy-start.7 = (f32[128]{0:T(128)S(1)}, f32[128]{0:T(128)}, u32[]{:S(2)}) copy-start(f32[128]{0:T(128)} %param.25) | copy-start | bytes 1540
  24.2 48.6 %copy-start.8 = (f32[128]{0:T(128)S(1)}, f32[128]{0:T(128)}, u32[]{:S(2)}) copy-start(f32[128]{0:T(128)} %param.24) | copy-start | bytes 1540
  56.4 13.0 %all-to-all-start = ((bf16[8,32,640]{2,1,0:T(8,128)(2,1)}), bf16[8,32,640]{2,1,0:T(8,128)(2,1)}, u32[]{:S(2)}, u32[]{:S(2)}) async-start(bf16[8,32,640]{2,1,0:T(8,128)(2,1)} %bitcast.2), calls=%async_computation | async-start | bytes 655360 | tf_op jit(solution)/shard_map/all_to_all | solution.py:125
  60.4 117.7 %reduce-scatter.2.cloned.1.call-start = ((), (), s32[]{:S(2)}) async-start(), calls=%async_computation.6 | async-start | bytes 1179648 | tf_op jit(solution)/shard_map/reduce_scatter | solution.py:130
  80.4 6.0 %copy-start.1 = (f32[4,32,8,4096]{3,2,1,0:T(8,128)}, f32[4,32,8,4096]{3,2,1,0:T(8,128)S(1)}, u32[]{:S(2)}) copy-start(f32[4,32,8,4096]{3,2,1,0:T(8,128)S(1)} %get-tuple-element.14) | copy-start | bytes 50331652
  97.7 17.0 %copy-start.6 = (s32[32,8]{0,1:T(8,128)S(1)}, s32[32,8]{0,1:T(8,128)}, u32[]{:S(2)}) copy-start(s32[32,8]{0,1:T(8,128)} %param.19) | copy-start | bytes 3076
  97.8 17.0 %copy-start.10 = (s32[16]{0:T(128)S(1)}, s32[16]{0:T(128)}, u32[]{:S(2)}) copy-start(s32[16]{0:T(128)} %param.21) | copy-start | bytes 196
  97.8 80.4 %copy-start.2 = (bf16[32,2048]{1,0:T(8,128)(2,1)S(1)}, bf16[32,2048]{1,0:T(8,128)(2,1)}, u32[]{:S(2)}) copy-start(bf16[32,2048]{1,0:T(8,128)(2,1)} %param.15) | copy-start | bytes 393220
  97.8 81.4 %copy-start.5 = (f32[2048]{0:T(1024)S(1)}, f32[2048]{0:T(1024)}, u32[]{:S(2)}) copy-start(f32[2048]{0:T(1024)} %param.23) | copy-start | bytes 24580
  213.3 7.2 %copy-start.4 = (s32[32,8]{0,1:T(8,128)S(1)}, s32[32,8]{0,1:T(8,128)}, u32[]{:S(2)}) copy-start(s32[32,8]{0,1:T(8,128)} %param.20) | copy-start | bytes 3076
  213.4 30.1 %copy-start.3 = (bf16[32,2048]{1,0:T(8,128)(2,1)S(1)}, bf16[32,2048]{1,0:T(8,128)(2,1)}, u32[]{:S(2)}) copy-start(bf16[32,2048]{1,0:T(8,128)(2,1)} %reduce-scatter.2.cloned.1.call-done) | copy-start | bytes 393220
  215.5 28.0 %all-to-all-start.3 = ((bf16[16,16,2048]{2,1,0:T(8,128)(2,1)}), bf16[16,16,2048]{2,1,0:T(8,128)(2,1)}, u32[]{:S(2)}, u32[]{:S(2)}) async-start(bf16[16,16,2048]{2,1,0:T(8,128)(2,1)} %bitcast.89), calls=%async_computation.4 | async-start | bytes 2097152 | tf_op jit(solution)/shard_map/all_to_all | solution.py:168
Sparse Core Ops, SparseCore 0:
  9.6 42.9 all-gather.1
  114.8 63.2 reduce-scatter.1
where the time goes:
time: 255 us; the launch traced here: 253 us
  waiting for transfers between devices  121 us (47%)
  blocking collectives  39.8 us (16%)
  matrix products  35.6 us (14%)
  local copies, waits for them, and re-layouts  19.6 us (8%)
  between operations  13.8 us (5%)
  other arithmetic  13.7 us (5%)
  starting transfers between devices  9.19 us (4%)
    reduce_scatter x1, waiting for transfers between devices, on_device(): lax.psum_scatter(jnp.dot(features, output_weight, preferred_element_type=...  61.7 us
    all_gather x1, waiting for transfers between devices, on_device(): lax.all_gather(normed, 'dev', axis=0, tiled=True)  28.1 us
    all_to_all x1, blocking collectives, on_device(): lax.all_to_all(outgoing, ('dev', 'sub'), split_axis=0, concat_axis=0, til...  28.1 us
    all_to_all x1, waiting for transfers between devices, on_device(): lax.all_to_all(computed, ('dev', 'sub'), split_axis=0, concat_axis=0, til...  22.7 us
    all_to_all x1, blocking collectives, on_device(): lax.all_to_all(attention, 'dev', split_axis=1, concat_axis=0, tiled=True)  11.6 us
    dot_general x1, matrix products, attend(): jnp.einsum('krgp,pkd->rkgd', weights, valued, preferred_element_type=jnp....  11.2 us
    all_to_all x1, waiting for transfers between devices, on_device(): lax.all_to_all(merged_cols, 'dev', split_axis=0, concat_axis=1, tiled=True)  8.66 us
    another operation x1, local copies, waits for them, and re-layouts, attend(): valued = value_rows.reshape(pool_size, kv_count, head_width)  6.97 us
  transfers between devices with their start and end apart: 4, of which 4 were waited for; matrix products, arithmetic and copies ran while one was open for 7% of the time, Pallas kernels for 0%

commit v1 on v0

v1 whole, which is shorter than its diff:
```python
import functools
import math

import jax
import jax.numpy as jnp
from jax import lax
from jax.experimental import pallas as pl
from jax.experimental.pallas import tpu as pltpu
from jax.sharding import PartitionSpec as P

HEADS = 32
KVH = 4
HD = 128

EPSILON = 1e-06
ROPE_BASE = 1000000.0
MESH = pl.DeviceIdType.MESH
VMEM = pl.BlockSpec(memory_space=pltpu.VMEM)


def norm_scale(values, scale_gain):
    mean_square = jnp.mean(values * values, axis=-1, keepdims=True)
    return values * lax.rsqrt(mean_square + EPSILON) * scale_gain


def rotate(values, position):
    half_width = values.shape[-1] // 2
    frequency = ROPE_BASE ** (-jnp.arange(half_width, dtype=jnp.float32) * 2.0 / values.shape[-1])
    angles = position.astype(jnp.float32)[:, None] * frequency[None, :]
    cosine = jnp.cos(angles)[:, None, :]
    sine_part = jnp.sin(angles)[:, None, :]
    first_half = values[..., :half_width]
    second_half = values[..., half_width:]
    return jnp.concatenate(
        [
            first_half * cosine - second_half * sine_part,
            second_half * cosine + first_half * sine_part,
        ],
        axis=-1,
    )


def place_of(dev, n):
    side = lax.rem(dev, 2)
    z = lax.div(dev, 2)
    return (1 - side) * z + side * (n - 1 - z)


def dev_at(place, n):
    place = lax.rem(place + 2 * n, n)
    side = lax.div(place, n // 2)
    return (1 - side) * (2 * place) + side * (2 * (n - 1 - place) + 1)


def greet(devs, subs=()):
    barrier = pltpu.get_barrier_semaphore()
    for dev in devs:
        pl.semaphore_signal(barrier, inc=1, device_id={"dev": dev}, device_id_type=MESH)
    for sub in subs:
        pl.semaphore_signal(barrier, inc=1, device_id={"sub": sub}, device_id_type=MESH)
    pl.semaphore_wait(barrier, len(devs) + len(subs))


def reach(n, way, half):
    return n // 2 if way == half else n // 2 - 1


def ring_gather(n, x_ref, slot, send_sem, recv_sem, on_block, on_half=None):
    me = lax.axis_index("dev")
    at = place_of(me, n)
    rows = x_ref.shape[0] // 2
    sides = (dev_at(at + 1, n), dev_at(at - 1, n))
    sent = []

    def send(src, origin, way, half, hop):
        copy = pltpu.make_async_remote_copy(
            src_ref=src,
            dst_ref=slot(origin, half),
            send_sem=send_sem.at[way, half, hop],
            recv_sem=recv_sem.at[way, half, hop],
            device_id={"dev": sides[way]},
            device_id_type=MESH,
        )
        copy.start()
        sent.append(copy)

    for half in range(2):
        for way in range(2):
            if reach(n, way, half) >= 1:
                send(x_ref.at[pl.ds(half * rows, rows)], me, way, half, 0)
    on_block(0, (me,))
    for hop in range(1, n // 2 + 1):
        origins = (dev_at(at - hop, n), dev_at(at + hop, n))
        for half in range(2):
            for way in range(2):
                if hop > reach(n, way, half):
                    continue
                origin = origins[way]
                here = slot(origin, half)
                pltpu.make_async_remote_copy(
                    src_ref=here,
                    dst_ref=here,
                    send_sem=send_sem.at[way, half, hop - 1],
                    recv_sem=recv_sem.at[way, half, hop - 1],
                    device_id={"dev": sides[way]},
                    device_id_type=MESH,
                ).wait_recv()
                if hop < reach(n, way, half):
                    send(here, origin, way, half, hop)
                if on_half is not None:
                    on_half(origin, half)
        on_block(hop, origins[:1] if 2 * hop == n else origins)
    return sent


def ring_reduce(n, part, rows, here, there, send_sem, recv_sem, out_ref):
    at = place_of(lax.axis_index("dev"), n)
    sides = (dev_at(at + 1, n), dev_at(at - 1, n))
    sent = []
    for away in range(n // 2, -1, -1):
        both = part(away, (dev_at(at + away, n), dev_at(at - away, n)))
        for half in range(2):
            total = both[0][half * rows : (half + 1) * rows] if away == 0 else None
            for way in range(2):
                far = reach(n, way, half)
                if away > far:
                    continue
                value = total if away == 0 else both[way][half * rows : (half + 1) * rows]
                if away < far:
                    pltpu.make_async_remote_copy(
                        src_ref=there.at[way, half, away],
                        dst_ref=there.at[way, half, away],
                        send_sem=send_sem.at[way, half, away],
                        recv_sem=recv_sem.at[way, half, away],
                        device_id={"dev": sides[way]},
                        device_id_type=MESH,
                    ).wait_recv()
                    value = value + there[way, half, away].astype(jnp.float32)
                if away == 0:
                    total = value
                    continue
                here[way, half, away - 1] = value.astype(here.dtype)
                copy = pltpu.make_async_remote_copy(
                    src_ref=here.at[way, half, away - 1],
                    dst_ref=there.at[way, half, away - 1],
                    send_sem=send_sem.at[way, half, away - 1],
                    recv_sem=recv_sem.at[way, half, away - 1],
                    device_id={"dev": sides[way]},
                    device_id_type=MESH,
                )
                copy.start()
                sent.append(copy)
            if away == 0:
                out_ref[half * rows : (half + 1) * rows, :] = total
    return sent


def others(n):
    me = lax.axis_index("dev")
    return [lax.rem(me + step, n) for step in range(1, n)]


def project_kernel(n, x_ref, w_ref, out_ref, held, mine, back, send_sem, recv_sem, back_send, back_recv):
    me = lax.axis_index("dev")
    at = place_of(me, n)
    rows = x_ref.shape[0]
    half_rows = rows // 2
    greet(others(n))
    waiting = []
    returned = []

    def post():
        for dev, lane in waiting:
            copy = pltpu.make_async_remote_copy(
                src_ref=mine.at[lane],
                dst_ref=back.at[lane],
                send_sem=back_send.at[lane],
                recv_sem=back_recv.at[lane],
                device_id={"dev": dev},
                device_id_type=MESH,
            )
            copy.start()
            returned.append(copy)
        waiting.clear()

    def on_block(hop, devs):
        if hop == 0:
            block = x_ref[...]
        else:
            block = jnp.concatenate([held[dev] for dev in devs], axis=0)
        product = jnp.dot(block, w_ref[...], preferred_element_type=jnp.float32).astype(mine.dtype)
        post()
        for index, dev in enumerate(devs):
            lane = hop if index == 0 else n - hop
            mine[lane] = product[index * rows : (index + 1) * rows]
            if hop > 0:
                waiting.append((dev, lane))

    sent = ring_gather(
        n,
        x_ref,
        lambda dev, half: held.at[dev, pl.ds(half * half_rows, half_rows)],
        send_sem,
        recv_sem,
        on_block,
    )
    post()
    out_ref[me] = mine[0]
    for copy in returned:
        copy.wait_recv()
    for lane in range(1, n):
        out_ref[dev_at(at + lane, n)] = back[lane]
    for copy in sent + returned:
        copy.wait_send()


def project(n, x, w, collective_id):
    rows, width = x.shape
    columns = w.shape[1]
    sems = pltpu.SemaphoreType.DMA((2, 2, n // 2))
    lanes = pltpu.SemaphoreType.DMA((n,))
    return pl.pallas_call(
        functools.partial(project_kernel, n),
        out_shape=jax.ShapeDtypeStruct((n, rows, columns), jnp.bfloat16),
        in_specs=[VMEM] * 2,
        out_specs=VMEM,
        scratch_shapes=[
            pltpu.VMEM((n, rows, width), x.dtype),
            pltpu.VMEM((n, rows, columns), jnp.bfloat16),
            pltpu.VMEM((n, rows, columns), jnp.bfloat16),
            sems,
            sems,
            lanes,
            lanes,
        ],
        compiler_params=pltpu.CompilerParams(collective_id=collective_id, has_side_effects=True),
        name="project",
    )(x, w)


def attend_kernel(tile, q_ref, nk_ref, nv_ref, first_ref, count_ref, k_ref, v_ref, out_ref, kept):
    scale = 1.0 / math.sqrt(q_ref.shape[2])
    q = q_ref[0]
    lines, width = q.shape
    requests = nk_ref.shape[1]
    fan = lines // requests

    def spread(values):
        return jnp.broadcast_to(values[:, None, :], (requests, fan, width)).reshape(lines, width)

    new_key = spread(nk_ref[0].astype(jnp.float32))
    new_value = spread(nv_ref[0].astype(jnp.float32))
    own = jnp.sum(q.astype(jnp.float32) * new_key, axis=1, keepdims=True)
    first = first_ref[...]
    last = first + count_ref[...]
    peak = own
    tiles = k_ref.shape[1] // tile
    lane = lax.broadcasted_iota(jnp.int32, (1, tile), 1)
    for index in range(tiles):
        keys = k_ref[0, index * tile : (index + 1) * tile]
        score = lax.dot_general(q, keys, (((1,), (1,)), ((), ())), preferred_element_type=jnp.float32)
        position = lane + index * tile
        inside = (position >= first) & (position < last)
        score = jnp.where(inside, score, -1e30)
        kept[index] = score
        peak = jnp.maximum(peak, jnp.max(score, axis=1, keepdims=True))
    own_raised = jnp.exp((own - peak) * scale)
    total = own_raised
    mixed = own_raised * new_value
    for index in range(tiles):
        raised = jnp.exp((kept[index] - peak) * scale)
        total = total + jnp.sum(raised, axis=1, keepdims=True)
        mixed = mixed + jnp.dot(
            raised.astype(jnp.bfloat16),
            v_ref[0, index * tile : (index + 1) * tile],
            preferred_element_type=jnp.float32,
        )
    out_ref[0] = (mixed / total).astype(out_ref.dtype)


def attend(queries, new_keys, new_values, key_cache, value_cache, lengths):
    rows, heads, width = queries.shape
    kv = new_keys.shape[1]
    fan = heads // kv
    pool = key_cache.shape[1]
    tile = math.gcd(pool, 1024)
    lines = rows * fan
    q = queries.reshape(rows, kv, fan, width).transpose(1, 0, 2, 3).reshape(kv, lines, width)
    end = jnp.cumsum(lengths)
    count = jnp.repeat(lengths, fan)[:, None]
    first = jnp.repeat(end - lengths, fan)[:, None]
    by_head = lambda *shape: pl.BlockSpec((1,) + shape, lambda head: (head, 0, 0))
    whole = pl.BlockSpec((lines, 1), lambda head: (0, 0))
    cache = pl.BlockSpec((1, pool, width), lambda head: (0, 0, head))
    out = pl.pallas_call(
        functools.partial(attend_kernel, tile),
        grid=(kv,),
        out_shape=jax.ShapeDtypeStruct((kv, lines, width), jnp.bfloat16),
        in_specs=[by_head(lines, width), by_head(rows, width), by_head(rows, width), whole, whole, cache, cache],
        out_specs=by_head(lines, width),
        scratch_shapes=[pltpu.VMEM((pool // tile, lines, tile), jnp.float32)],
        name="attend",
    )(q, new_keys.transpose(1, 0, 2), new_values.transpose(1, 0, 2), first, count, key_cache, value_cache)
    return out.reshape(kv, rows, fan, width).transpose(1, 0, 2, 3).reshape(rows, heads * width)


def output_kernel(n, a_ref, w_ref, out_ref, held, here, there, send_sem, recv_sem, move_send, move_recv):
    at = place_of(lax.axis_index("dev"), n)
    me = lax.axis_index("dev")
    rows = a_ref.shape[1]
    greet(others(n))
    moves = {}
    order = [n // 2]
    for away in range(n // 2 - 1, 0, -1):
        order += [away, n - away]
    for lane in order:
        copy = pltpu.make_async_remote_copy(
            src_ref=a_ref.at[dev_at(at - lane, n)],
            dst_ref=held.at[lane],
            send_sem=move_send.at[lane],
            recv_sem=move_recv.at[lane],
            device_id={"dev": dev_at(at - lane, n)},
            device_id_type=MESH,
        )
        copy.start()
        moves[lane] = copy

    def part(away, devs):
        lanes = (away,) if away == 0 or 2 * away == n else (away, n - away)
        if away == 0:
            features = a_ref[me]
        else:
            for lane in lanes:
                moves[lane].wait_recv()
            features = jnp.concatenate([held[lane] for lane in lanes], axis=0)
        product = jnp.dot(features, w_ref[...], preferred_element_type=jnp.float32)
        return (product[:rows], product[-rows:])

    sent = ring_reduce(n, part, rows // 2, here, there, send_sem, recv_sem, out_ref)
    for copy in sent + list(moves.values()):
        copy.wait_send()


def output(n, a, w, collective_id):
    _, rows, depth = a.shape
    width = w.shape[1]
    sems = pltpu.SemaphoreType.DMA((2, 2, n // 2))
    lanes = pltpu.SemaphoreType.DMA((n,))
    return pl.pallas_call(
        functools.partial(output_kernel, n),
        out_shape=jax.ShapeDtypeStruct((rows, width), jnp.float32),
        in_specs=[VMEM] * 2,
        out_specs=VMEM,
        scratch_shapes=[
            pltpu.VMEM((n, rows, depth), a.dtype),
            pltpu.VMEM((2, 2, n // 2, rows // 2, width), jnp.bfloat16),
            pltpu.VMEM((2, 2, n // 2, rows // 2, width), jnp.bfloat16),
            sems,
            sems,
            lanes,
            lanes,
        ],
        compiler_params=pltpu.CompilerParams(collective_id=collective_id, has_side_effects=True),
        name="output",
    )(a, w)


def gather_kernel(n, s, x_ref, out_ref, send_sem, recv_sem, pair_send, pair_recv):
    me = lax.axis_index("dev")
    at = place_of(me, n)
    sub = lax.axis_index("sub")
    rows = x_ref.shape[0] // 2
    partners = [lax.rem(sub + step, s) for step in range(1, s)]
    greet((dev_at(at + 1, n), dev_at(at - 1, n)), partners)
    pairs = []

    def share(src, origin, half):
        for step, partner in enumerate(partners):
            copy = pltpu.make_async_remote_copy(
                src_ref=src,
                dst_ref=out_ref.at[origin, sub, pl.ds(half * rows, rows)],
                send_sem=pair_send.at[step, origin, half],
                recv_sem=pair_recv.at[step, origin, half],
                device_id={"sub": partner},
                device_id_type=MESH,
            )
            copy.start()
            pairs.append((copy, step, origin, half))

    slot = lambda dev, half: out_ref.at[dev, sub, pl.ds(half * rows, rows)]

    def on_block(hop, devs):
        if hop == 0:
            for half in range(2):
                share(x_ref.at[pl.ds(half * rows, rows)], me, half)
            out_ref[me, sub] = x_ref[...]

    sent = ring_gather(
        n, x_ref, slot, send_sem, recv_sem, on_block, lambda origin, half: share(slot(origin, half), origin, half)
    )
    for copy, step, origin, half in pairs:
        came = out_ref.at[origin, lax.rem(sub + s - step - 1, s), pl.ds(half * rows, rows)]
        pltpu.make_async_remote_copy(
            src_ref=came,
            dst_ref=came,
            send_sem=pair_send.at[step, origin, half],
            recv_sem=pair_recv.at[step, origin, half],
            device_id={"sub": partners[step]},
            device_id_type=MESH,
        ).wait_recv()
    for copy in sent + [entry[0] for entry in pairs]:
        copy.wait_send()


def gather(n, s, x, collective_id):
    rows, width = x.shape
    sems = pltpu.SemaphoreType.DMA((2, 2, n // 2))
    pair = pltpu.SemaphoreType.DMA((max(s - 1, 1), n, 2))
    return pl.pallas_call(
        functools.partial(gather_kernel, n, s),
        out_shape=jax.ShapeDtypeStruct((n, s, rows, width), x.dtype),
        in_specs=[VMEM],
        out_specs=VMEM,
        scratch_shapes=[sems, sems, pair, pair],
        compiler_params=pltpu.CompilerParams(collective_id=collective_id, has_side_effects=True),
        name="gather",
    )(x)


def combine_kernel(n, s, p_ref, out_ref, near, here, there, send_sem, recv_sem, pair_send, pair_recv):
    me = lax.axis_index("dev")
    at = place_of(me, n)
    sub = lax.axis_index("sub")
    rows = p_ref.shape[2]
    partners = [lax.rem(sub + step, s) for step in range(1, s)]
    greet((dev_at(at + 1, n), dev_at(at - 1, n)), partners)
    order = [n // 2]
    for away in range(n // 2 - 1, 0, -1):
        order += [away, n - away]
    order.append(0)
    pairs = {}
    for lane in order:
        for step, partner in enumerate(partners):
            copy = pltpu.make_async_remote_copy(
                src_ref=p_ref.at[dev_at(at + lane, n), partner],
                dst_ref=near.at[step, lane],
                send_sem=pair_send.at[step, lane],
                recv_sem=pair_recv.at[step, lane],
                device_id={"sub": partner},
                device_id_type=MESH,
            )
            copy.start()
            pairs[step, lane] = copy

    def one(lane):
        value = p_ref[dev_at(at + lane, n), sub].astype(jnp.float32)
        for step in range(s - 1):
            pairs[step, lane].wait_recv()
            value = value + near[step, lane].astype(jnp.float32)
        return value

    def part(away, devs):
        front = one(away)
        if away == 0 or 2 * away == n:
            return (front, front)
        return (front, one(n - away))

    sent = ring_reduce(n, part, rows // 2, here, there, send_sem, recv_sem, out_ref)
    for copy in sent + list(pairs.values()):
        copy.wait_send()


def combine(n, s, parts, collective_id):
    _, _, rows, width = parts.shape
    sems = pltpu.SemaphoreType.DMA((2, 2, n // 2))
    pair = pltpu.SemaphoreType.DMA((max(s - 1, 1), n))
    return pl.pallas_call(
        functools.partial(combine_kernel, n, s),
        out_shape=jax.ShapeDtypeStruct((rows, width), jnp.float32),
        in_specs=[VMEM],
        out_specs=VMEM,
        scratch_shapes=[
            pltpu.VMEM((max(s - 1, 1), n, rows, width), jnp.bfloat16),
            pltpu.VMEM((2, 2, n // 2, rows // 2, width), jnp.bfloat16),
            pltpu.VMEM((2, 2, n // 2, rows // 2, width), jnp.bfloat16),
            sems,
            sems,
            pair,
            pair,
        ],
        compiler_params=pltpu.CompilerParams(collective_id=collective_id, has_side_effects=True),
        name="combine",
    )(parts)


def on_device(
    n,
    s,
    hidden,
    lengths,
    key_cache,
    value_cache,
    expert_ids,
    gate_codes,
    expert_device,
    attention_gain,
    mixture_gain,
    query_gain,
    key_gain,
    project_weight,
    output_weight,
    expert_gate_up,
    expert_down,
):
    rows, width = hidden.shape
    normed = norm_scale(hidden.astype(jnp.float32), attention_gain).astype(jnp.bfloat16)
    merged = project(n, normed, project_weight, 0)
    merged = merged.transpose(1, 0, 2).reshape(rows, -1)
    position = lengths.reshape(rows)
    split = HEADS * HD
    new = split + KVH * HD
    queries = merged[:, :split].astype(jnp.float32).reshape(rows, HEADS, HD)
    queries = rotate(norm_scale(queries, query_gain), position).astype(jnp.bfloat16)
    new_keys = merged[:, split:new].astype(jnp.float32).reshape(rows, KVH, HD)
    new_keys = rotate(norm_scale(new_keys, key_gain), position).astype(jnp.bfloat16)
    new_values = merged[:, new:].reshape(rows, KVH, HD)
    attention = attend(queries, new_keys, new_values, key_cache, value_cache, position)
    depth = output_weight.shape[0]
    projected = output(n, attention.reshape(rows, n, depth).transpose(1, 0, 2), output_weight, 1)
    residual = hidden.astype(jnp.float32) + projected
    mixture_in = norm_scale(residual, mixture_gain).astype(jnp.bfloat16)

    experts = expert_device.shape[0]
    numbers = jnp.arange(experts, dtype=jnp.int32)
    at_slot = (expert_device[:, None] == numbers[None, :])[None, None]
    named = (expert_ids[:, :, None] == numbers[None, None, :])[..., None]
    codes = jnp.sum(jnp.where(named & at_slot, gate_codes[:, :, None, None], 0), axis=(1, 2))
    coded = jnp.concatenate([codes // 32, codes % 32], axis=1).astype(jnp.bfloat16)
    extra = -(-coded.shape[1] // 128) * 128
    coded = jnp.pad(coded, ((0, 0), (0, extra - coded.shape[1])))
    everyone = gather(n, s, jnp.concatenate([mixture_in, coded], axis=1), 2)
    flat = everyone.reshape(n * s * rows, width + extra)
    arrived = flat[:, :width]
    tail = flat[:, width:].astype(jnp.float32)
    all_codes = tail[:, :experts] * 32.0 + tail[:, experts : 2 * experts]
    slot = lax.axis_index("dev") * s + lax.axis_index("sub")
    mine = jnp.sum(jnp.where(numbers[None, :] == slot, all_codes, 0.0), axis=1, keepdims=True)
    share = mine / jnp.sum(all_codes, axis=1, keepdims=True)
    both_parts = jnp.dot(arrived, expert_gate_up[0], preferred_element_type=jnp.float32)
    inner = expert_down.shape[1]
    units = (jax.nn.silu(both_parts[:, :inner]) * both_parts[:, inner:]).astype(jnp.bfloat16)
    result = jnp.dot(units, expert_down[0], preferred_element_type=jnp.float32).astype(jnp.bfloat16)
    parts = jnp.where(mine > 0.0, result.astype(jnp.float32) * share, 0.0).astype(jnp.bfloat16)
    routed = combine(n, s, parts.reshape(n, s, rows, width), 3)
    return (residual + routed).astype(jnp.bfloat16)


def solution(mesh):
    return jax.shard_map(
        functools.partial(on_device, mesh.shape["dev"], mesh.shape["sub"]),
        mesh=mesh,
        in_specs=(
            P(("groups", "dev", "sub"), None),
            P(("groups", "dev", "sub"), None),
            P(("groups", "dev", "sub"), None, None),
            P(("groups", "dev", "sub"), None, None),
            P(("groups", "dev", "sub"), None),
            P(("groups", "dev", "sub"), None),
            P(),
            P(),
            P(),
            P(),
            P(),
            P(None, "dev"),
            P("dev", None),
            P(("dev", "sub"), None, None),
            P(("dev", "sub"), None, None),
        ),
        out_specs=P(("groups", "dev", "sub"), None),
        check_vma=False,
    )
```

time: 255 us -> 154 us (0.60)
  waiting for transfers between devices: 121 us -> 0 us
  Pallas kernels: 0 us -> 110 us
  blocking collectives: 39.8 us -> 0 us
  matrix products: 35.6 us -> 9.4 us
  between operations: 13.8 us -> 0.23 us
  starting transfers between devices: 9.19 us -> 0 us
  local copies, waits for them, and re-layouts: 19.6 us -> 11.3 us
  other arithmetic: 13.7 us -> 21.9 us
    pallas_call x0 -> x5, Pallas kernels: none -> 110 us  [the longest x1 32.1 us: project(): pl.pallas_call(functools.partial(project_kernel, n), out_shape=jax.ShapeD...]
    reduce_scatter x1 -> x0, waiting for transfers between devices: 61.7 us -> none  [on_device(): lax.psum_scatter(jnp.dot(features, output_weight, preferred_element_type=...]
    all_to_all x2 -> x0, blocking collectives: 39.8 us -> none  [the longest x1 28.1 us: on_device(): lax.all_to_all(outgoing, ('dev', 'sub'), split_axis=0, concat_axis=0, til...]
    all_to_all x2 -> x0, waiting for transfers between devices: 31.3 us -> none  [the longest x1 22.7 us: on_device(): lax.all_to_all(computed, ('dev', 'sub'), split_axis=0, concat_axis=0, til...]
    all_gather x1 -> x0, waiting for transfers between devices: 28.1 us -> none  [on_device(): lax.all_gather(normed, 'dev', axis=0, tiled=True)]
    dot_general x9 -> x2, matrix products: 35.6 us -> 9.4 us  [the longest x1 6.17 us: on_device(): jnp.dot(arrived, expert_gate_up[0], preferred_element_type=jnp.float32)]
    another operation x4 -> x5, local copies, waits for them, and re-layouts: 14.6 us -> 4.78 us  [the longest x2 2.57 us: on_device(): attention.reshape(rows, n, depth).transpose(1, 0, 2)]
    all_to_all x2 -> x0, starting transfers between devices: 9.15 us -> none  [the longest x1 5.08 us: on_device(): lax.all_to_all(computed, ('dev', 'sub'), split_axis=0, concat_axis=0, til...]
  transfers between devices with their start and end apart: 4 -> 0, of which waited for: 4 -> 0; matrix products, arithmetic and copies ran while one was open for 7% -> 0% of each run, Pallas kernels for 0% -> 0%
where the time goes in v1:
time: 154 us; the launch traced here: 153 us
  Pallas kernels  110 us (71%)
  other arithmetic  21.9 us (14%)
  local copies, waits for them, and re-layouts  11.3 us (7%)
  matrix products  9.4 us (6%)
    pallas_call x1, Pallas kernels, project(): pl.pallas_call(functools.partial(project_kernel, n), out_shape=jax.ShapeD...  32.1 us
    pallas_call x1, Pallas kernels, output(): pl.pallas_call(functools.partial(output_kernel, n), out_shape=jax.ShapeDt...  24.5 us
    pallas_call x1, Pallas kernels, gather(): pl.pallas_call(functools.partial(gather_kernel, n, s), out_shape=jax.Shap...  20.7 us
    pallas_call x1, Pallas kernels, combine(): pl.pallas_call(functools.partial(combine_kernel, n, s), out_shape=jax.Sha...  19.7 us
    pallas_call x1, Pallas kernels, attend(): pl.pallas_call(functools.partial(attend_kernel, tile), grid=(kv,), out_sh...  13 us
    dot_general x1, matrix products, on_device(): jnp.dot(arrived, expert_gate_up[0], preferred_element_type=jnp.float32)  6.17 us
    reduce_sum x4, other arithmetic, norm_scale(): mean_square = jnp.mean(values * values, axis=-1, keepdims=True)  3.89 us
    dot_general x1, matrix products, on_device(): jnp.dot(units, expert_down[0], preferred_element_type=jnp.float32)  3.23 us

profile of v1, /device:TPU:0, one launch (start us, length us, event | category | flops | bytes accessed | tf_op | source)
XLA Modules:
  0.0 152.9 jit_solution(13882117315416522954)
XLA Ops:
  0.6 1.0 bitcast_convert_fusion
  1.6 1.0 fusion.13
  4.1 0.9 select_reduce_fusion
  10.4 1.7 %fusion.15.x_ref = bf16[32,2048]{1,0:T(8,128)(2,1)} fusion(bf16[32,2048]{1,0:T(8,128)(2,1)} %param.15, f32[2048]{0:T(1024)} %param.22, f32[32]{0:T(128)S(1)} %add_rsqrt_fusion.3), kind=kLoop, calls=%fused_computation.21 | loop fusion | flops 262144 | bytes 270464 | tf_op jit(solution)/shard_map/convert_element_type | solution.py:516
  12.0 32.1 %project.1 = bf16[8,32,640]{2,1,0:T(8,128)(2,1)} custom-call(bf16[32,2048]{1,0:T(8,128)(2,1)} %fusion.15.x_ref, bf16[2048,640]{1,0:T(8,128)(2,1)} %w_ref.2), custom_call_target="tpu_custom_call" | custom-call | tf_op jit(solution)/shard_map/project/pallas_call | solution.py:222
  44.1 1.0 copy.72
  46.4 1.5 reshape.213
  47.8 1.6 %multiply_reduce_fusion.2 = f32[32,4]{1,0:T(8,128)} fusion(f32[32,4,128]{2,1,0:T(4,128)} %reshape.213), kind=kLoop, calls=%fused_computation.42 | loop fusion | flops 32640 | bytes 66048 | tf_op jit(solution)/shard_map/reduce_sum | solution.py:22
  49.4 1.4 copy.58
  54.1 0.9 multiply_multiply_fusion
  55.2 0.8 copy_bitcast_fusion.2.q_ref
  56.0 13.0 %attend.1 = bf16[4,256,128]{2,1,0:T(8,128)(2,1)} custom-call(bf16[4,256,128]{2,1,0:T(8,128)(2,1)} %copy_bitcast_fusion.2.q_ref, bf16[4,32,128]{2,1,0:T(8,128)(2,1)} %maximum_bitcast_fusion.1.nk_ref, bf16[4,32,128]{2,1,0:T(8,128)(2,1)} %bitcast.66, s32[256,1]{1,0:T(8,128)} %broadcast_in_dim_reshape.8.first_ref, s32[256,1]{1,0:T(8,128)} %broadcast_in_dim_reshape.9.count_ref, ...), custom_call_target="tpu_custom_call" | custom-call | tf_op jit(solution)/shard_map/attend/pallas_call | solution.py:295
  69.1 1.0 copy_bitcast_fusion.1
  70.1 0.9 reshape_reshape.3
  71.0 1.7 %copy.79 = bf16[32,8,512]{2,0,1:T(8,128)(2,1)} copy(bf16[32,8,512]{2,1,0:T(8,128)(2,1)} %reshape_reshape.3) | data formatting | bytes 524288 | tf_op jit(solution)/shard_map/reshape;reshape | solution.py:529
  72.7 24.5 %output.1 = f32[32,2048]{1,0:T(8,128)} custom-call(bf16[8,32,512]{2,1,0:T(8,128)(2,1)} %bitcast.65, bf16[512,2048]{1,0:T(8,128)(2,1)} %w_ref.3), custom_call_target="tpu_custom_call" | custom-call | tf_op jit(solution)/shard_map/output/pallas_call | solution.py:349
  97.2 1.1 multiply_reduce_fusion.1
  98.4 1.0 multiply_convert_fusion
  100.1 20.7 %gather.1 = bf16[8,2,32,2176]{3,2,1,0:T(8,128)(2,1)} custom-call(bf16[32,2176]{1,0:T(8,128)(2,1)} %pad_maximum_fusion.x_ref), custom_call_target="tpu_custom_call" | custom-call | tf_op jit(solution)/shard_map/gather/pallas_call | solution.py:419
  120.8 0.9 slice_convert_fusion
  122.1 6.2 %fusion = f32[512,1536]{1,0:T(8,128)S(1)} fusion(bf16[1,2048,1536]{2,1,0:T(8,128)(2,1)} %param.28, bf16[512,2176]{1,0:T(8,128)(2,1)} %bitcast.60), kind=kOutput, calls=%fused_computation | convolution fusion | flops 3221225472 | bytes 11534336 | tf_op jit(solution)/shard_map/dot_general | solution.py:549
  128.3 3.2 %select_convert_fusion = bf16[512,2048]{1,0:T(8,128)(2,1)} fusion(bf16[1,768,2048]{2,1,0:T(8,128)(2,1)S(1)} %copy-done, f32[512]{0:T(512)S(1)} %div.61, pred[512]{0:T(512)(128)(4,1)S(1)} %broadcast_compare_fusion, f32[512,1536]{1,0:T(8,128)S(1)} %fusion), kind=kOutput, calls=%fused_computation.2 | convolution fusion | flops 1618214912 | bytes 8391168 | tf_op jit(solution)/shard_map/dot_general | solution.py:552
  131.5 19.7 %combine.1 = f32[32,2048]{1,0:T(8,128)} custom-call(bf16[8,2,32,2048]{3,2,1,0:T(8,128)(2,1)} %bitcast.61), custom_call_target="tpu_custom_call" | custom-call | tf_op jit(solution)/shard_map/combine/pallas_call | solution.py:477
  151.2 1.6 %add_convert_fusion.1 = bf16[32,2048]{1,0:T(8,128)(2,1)} fusion(f32[32,2048]{1,0:T(8,128)} %combine.1, f32[32,2048]{1,0:T(8,128)S(1)} %copy-done.1, bf16[32,2048]{1,0:T(8,128)(2,1)S(1)} %copy-done.2), kind=kLoop, calls=%fused_computation.30 | loop fusion | flops 262144 | bytes 786432 | tf_op jit(solution)/shard_map/convert_element_type | solution.py:555
  (47 shorter events, 13.2 us)
Async XLA Ops:
  0.0 128.3 %copy-start = (bf16[1,768,2048]{2,1,0:T(8,128)(2,1)S(1)}, bf16[1,768,2048]{2,1,0:T(8,128)(2,1)}, u32[]{:S(2)}) copy-start(bf16[1,768,2048]{2,1,0:T(8,128)(2,1)} %param.29) | copy-start | bytes 9437188
  50.8 4.2 %copy-start.3 = (f32[32,64]{1,0:T(8,128)S(1)}, f32[32,64]{1,0:T(8,128)}, u32[]{:S(2)}) copy-start(f32[32,64]{1,0:T(8,128)} %get-tuple-element.17) | copy-start | bytes 24580
  69.1 28.1 %copy-start.2 = (bf16[32,2048]{1,0:T(8,128)(2,1)S(1)}, bf16[32,2048]{1,0:T(8,128)(2,1)}, u32[]{:S(2)}) copy-start(bf16[32,2048]{1,0:T(8,128)(2,1)} %param.15) | copy-start | bytes 393220
  69.1 29.3 %copy-start.5 = (f32[2048]{0:T(1024)S(1)}, f32[2048]{0:T(1024)}, u32[]{:S(2)}) copy-start(f32[2048]{0:T(1024)} %param.23) | copy-start | bytes 24580
  69.1 30.3 %copy-start.4 = (bf16[32,128]{1,0:T(8,128)(2,1)S(1)}, bf16[32,128]{1,0:T(8,128)(2,1)}, u32[]{:S(2)}) copy-start(bf16[32,128]{1,0:T(8,128)(2,1)} %fusion.27) | copy-start | bytes 24580
  72.7 49.1 %copy-start.6 = (pred[16]{0:T(512)(128)(4,1)S(1)}, pred[16]{0:T(512)(128)(4,1)}, u32[]{:S(2)}) copy-start(pred[16]{0:T(512)(128)(4,1)} %iota_compare_fusion.3) | copy-start | bytes 52
  128.3 22.9 %copy-start.1 = (f32[32,2048]{1,0:T(8,128)S(1)}, f32[32,2048]{1,0:T(8,128)}, u32[]{:S(2)}) copy-start(f32[32,2048]{1,0:T(8,128)} %output.1) | copy-start | bytes 786436

commit v2 on v1

v2 whole, which is shorter than its diff:
```python
import functools
import math

import jax
import jax.numpy as jnp
import numpy as np
from jax import lax
from jax.experimental import pallas as pl
from jax.experimental.pallas import tpu as pltpu
from jax.sharding import PartitionSpec as P

HEADS = 32
KVH = 4
HD = 128

EPSILON = 1e-06
ROPE_BASE = 1000000.0
MESH = pl.DeviceIdType.MESH
VMEM = pl.BlockSpec(memory_space=pltpu.VMEM)
ANY = pl.BlockSpec(memory_space=pl.ANY)


def norm_scale(values, scale_gain):
    mean_square = jnp.mean(values * values, axis=-1, keepdims=True)
    return values * lax.rsqrt(mean_square + EPSILON) * scale_gain


def place_of(dev, n):
    side = lax.rem(dev, 2)
    z = lax.div(dev, 2)
    return (1 - side) * z + side * (n - 1 - z)


def dev_at(place, n):
    place = lax.rem(place + 2 * n, n)
    side = lax.div(place, n // 2)
    return (1 - side) * (2 * place) + side * (2 * (n - 1 - place) + 1)


def greet(devs, subs=()):
    barrier = pltpu.get_barrier_semaphore()
    for dev in devs:
        pl.semaphore_signal(barrier, inc=1, device_id={"dev": dev}, device_id_type=MESH)
    for sub in subs:
        pl.semaphore_signal(barrier, inc=1, device_id={"sub": sub}, device_id_type=MESH)


def meet(count):
    pl.semaphore_wait(pltpu.get_barrier_semaphore(), count)


def reach(n, way, half):
    return n // 2 if way == half else n // 2 - 1


def ring_gather(n, x_ref, slot, send_sem, recv_sem, on_block, on_half=None):
    me = lax.axis_index("dev")
    at = place_of(me, n)
    rows = x_ref.shape[0] // 2
    sides = (dev_at(at + 1, n), dev_at(at - 1, n))
    sent = []

    def send(src, origin, way, half, hop):
        copy = pltpu.make_async_remote_copy(
            src_ref=src,
            dst_ref=slot(origin, half),
            send_sem=send_sem.at[way, half, hop],
            recv_sem=recv_sem.at[way, half, hop],
            device_id={"dev": sides[way]},
            device_id_type=MESH,
        )
        copy.start()
        sent.append(copy)

    for half in range(2):
        for way in range(2):
            if reach(n, way, half) >= 1:
                send(x_ref.at[pl.ds(half * rows, rows)], me, way, half, 0)
    on_block(0, (me,))
    for hop in range(1, n // 2 + 1):
        origins = (dev_at(at - hop, n), dev_at(at + hop, n))
        for half in range(2):
            for way in range(2):
                if hop > reach(n, way, half):
                    continue
                origin = origins[way]
                here = slot(origin, half)
                pltpu.make_async_remote_copy(
                    src_ref=here,
                    dst_ref=here,
                    send_sem=send_sem.at[way, half, hop - 1],
                    recv_sem=recv_sem.at[way, half, hop - 1],
                    device_id={"dev": sides[way]},
                    device_id_type=MESH,
                ).wait_recv()
                if hop < reach(n, way, half):
                    send(here, origin, way, half, hop)
                if on_half is not None:
                    on_half(origin, half)
        on_block(hop, origins[:1] if 2 * hop == n else origins)
    return sent


def ring_reduce(n, part, rows, here, there, send_sem, recv_sem, finish):
    at = place_of(lax.axis_index("dev"), n)
    sides = (dev_at(at + 1, n), dev_at(at - 1, n))
    sent = []
    for away in range(n // 2, -1, -1):
        both = part(away, (dev_at(at + away, n), dev_at(at - away, n)))
        for half in range(2):
            total = both[0][half * rows : (half + 1) * rows] if away == 0 else None
            for way in range(2):
                far = reach(n, way, half)
                if away > far:
                    continue
                value = total if away == 0 else both[way][half * rows : (half + 1) * rows]
                if away < far:
                    pltpu.make_async_remote_copy(
                        src_ref=there.at[way, half, away],
                        dst_ref=there.at[way, half, away],
                        send_sem=send_sem.at[way, half, away],
                        recv_sem=recv_sem.at[way, half, away],
                        device_id={"dev": sides[way]},
                        device_id_type=MESH,
                    ).wait_recv()
                    value = value + there[way, half, away].astype(jnp.float32)
                if away == 0:
                    total = value
                    continue
                here[way, half, away - 1] = value.astype(here.dtype)
                copy = pltpu.make_async_remote_copy(
                    src_ref=here.at[way, half, away - 1],
                    dst_ref=there.at[way, half, away - 1],
                    send_sem=send_sem.at[way, half, away - 1],
                    recv_sem=recv_sem.at[way, half, away - 1],
                    device_id={"dev": sides[way]},
                    device_id_type=MESH,
                )
                copy.start()
                sent.append(copy)
            if away == 0:
                finish(half, total)
    return sent


def others(n):
    me = lax.axis_index("dev")
    return [lax.rem(me + step, n) for step in range(1, n)]


def project_kernel(
    n, hidden_ref, gain_ref, rate_ref, length_ref, id_ref, code_ref, place_ref, w_hbm,
    out_ref, turn_ref, span_ref, coded_ref,
    x_ref, w_ref, held, mine, back, w_sem, send_sem, recv_sem, back_send, back_recv,
):
    me = lax.axis_index("dev")
    at = place_of(me, n)
    rows = x_ref.shape[0]
    half_rows = rows // 2
    load = pltpu.make_async_copy(w_hbm, w_ref, w_sem)
    load.start()
    greet(others(n))
    x_ref[...] = norm_scale(hidden_ref[...].astype(jnp.float32), gain_ref[...]).astype(x_ref.dtype)
    meet(n - 1)
    waiting = []
    returned = []

    def post():
        for dev, lane in waiting:
            copy = pltpu.make_async_remote_copy(
                src_ref=mine.at[lane],
                dst_ref=back.at[lane],
                send_sem=back_send.at[lane],
                recv_sem=back_recv.at[lane],
                device_id={"dev": dev},
                device_id_type=MESH,
            )
            copy.start()
            returned.append(copy)
        waiting.clear()

    def tables():
        across = lax.broadcasted_iota(jnp.int32, (rows, rows), 1)
        down = lax.broadcasted_iota(jnp.int32, (rows, rows), 0)
        lengths = jnp.broadcast_to(length_ref[...], (rows, rows))
        own = jnp.sum(jnp.where(across == down, lengths, 0), axis=1, keepdims=True)
        first = jnp.sum(jnp.where(across < down, lengths, 0), axis=1, keepdims=True)
        lanes = span_ref.shape[2]
        span_ref[0] = jnp.broadcast_to(first, (rows, lanes))
        span_ref[1] = jnp.broadcast_to(first + own, (rows, lanes))
        angles = own.astype(jnp.float32) * rate_ref[...]
        turn_ref[0] = jnp.cos(angles)
        side = lax.broadcasted_iota(jnp.int32, angles.shape, 1)
        sine = jnp.sin(angles)
        turn_ref[1] = jnp.where(side < lanes // 2, -sine, sine)
        experts = place_ref.shape[1]
        number = lax.broadcasted_iota(jnp.int32, (rows, experts), 1)
        lane = lax.broadcasted_iota(jnp.int32, (rows, coded_ref.shape[1]), 1)
        coded = jnp.zeros(lane.shape, jnp.int32)
        for choice in range(id_ref.shape[1]):
            named = number == id_ref[:, choice : choice + 1]
            holder = jnp.sum(jnp.where(named, place_ref[...], 0), axis=1, keepdims=True)
            code = code_ref[:, choice : choice + 1]
            coded = coded + jnp.where(lane == holder, code >> 5, 0)
            coded = coded + jnp.where(lane == holder + experts, code & 31, 0)
        coded_ref[...] = coded.astype(jnp.float32).astype(coded_ref.dtype)

    def on_block(hop, devs):
        if hop == 0:
            tables()
            load.wait()
            block = x_ref[...]
        else:
            block = jnp.concatenate([held[dev] for dev in devs], axis=0)
        product = jnp.dot(block, w_ref[...], preferred_element_type=jnp.float32).astype(mine.dtype)
        post()
        for index, dev in enumerate(devs):
            lane = hop if index == 0 else n - hop
            mine[lane] = product[index * rows : (index + 1) * rows]
            if hop > 0:
                waiting.append((dev, lane))

    sent = ring_gather(
        n,
        x_ref,
        lambda dev, half: held.at[dev, pl.ds(half * half_rows, half_rows)],
        send_sem,
        recv_sem,
        on_block,
    )
    post()
    out_ref[me] = mine[0]
    for copy in returned:
        copy.wait_recv()
    for lane in range(1, n):
        out_ref[dev_at(at + lane, n)] = back[lane]
    for copy in sent + returned:
        copy.wait_send()


def project(n, hidden, gain, lengths, ids, codes, places, w, collective_id):
    rows, width = hidden.shape
    columns = w.shape[1]
    sems = pltpu.SemaphoreType.DMA((2, 2, n // 2))
    lanes = pltpu.SemaphoreType.DMA((n,))
    rates = ROPE_BASE ** (-np.arange(HD // 2) * 2.0 / HD)
    rates = jnp.asarray(np.concatenate([rates, rates])[None, :], jnp.float32)
    extra = -(-2 * places.shape[0] // 128) * 128
    return pl.pallas_call(
        functools.partial(project_kernel, n),
        out_shape=(
            jax.ShapeDtypeStruct((n, rows, columns), jnp.bfloat16),
            jax.ShapeDtypeStruct((2, rows, HD), jnp.float32),
            jax.ShapeDtypeStruct((2, rows, HD), jnp.int32),
            jax.ShapeDtypeStruct((rows, extra), jnp.bfloat16),
        ),
        in_specs=[VMEM] * 7 + [ANY],
        out_specs=[VMEM] * 4,
        scratch_shapes=[
            pltpu.VMEM((rows, width), jnp.bfloat16),
            pltpu.VMEM(w.shape, w.dtype),
            pltpu.VMEM((n, rows, width), jnp.bfloat16),
            pltpu.VMEM((n, rows, columns), jnp.bfloat16),
            pltpu.VMEM((n, rows, columns), jnp.bfloat16),
            pltpu.SemaphoreType.DMA,
            sems,
            sems,
            lanes,
            lanes,
        ],
        compiler_params=pltpu.CompilerParams(collective_id=collective_id, has_side_effects=True),
        name="project",
    )(hidden, gain[None, :], rates, lengths, ids, codes, places[None, :], w)


def attend_kernel(
    tile, merged_ref, turn_ref, span_ref, query_gain_ref, key_gain_ref, k_hbm, v_hbm,
    out_ref, k_ref, v_ref, kept, k_sem, v_sem,
):
    width = HD
    loads = []
    for head in range(KVH):
        columns = pl.ds(head * width, width)
        for source, target, sem in ((k_hbm, k_ref, k_sem), (v_hbm, v_ref, v_sem)):
            copy = pltpu.make_async_copy(source.at[0, :, columns], target.at[head], sem.at[head])
            copy.start()
            loads.append(copy)
    rows = merged_ref.shape[1]
    scale = 1.0 / math.sqrt(width)
    fan = HEADS // KVH
    lines = rows * fan
    per_in = merged_ref.shape[2]
    per_out = out_ref.shape[2]

    def columns_of(head):
        pieces = []
        low, high = head * width, (head + 1) * width
        while low < high:
            dev, start = low // per_in, low % per_in
            count = min(high - low, per_in - start)
            pieces.append(merged_ref[dev, :, start : start + count].astype(jnp.float32))
            low += count
        return pieces[0] if len(pieces) == 1 else jnp.concatenate(pieces, axis=1)

    def turned(head, gain):
        values = norm_scale(columns_of(head), gain)
        swapped = jnp.concatenate([values[:, width // 2 :], values[:, : width // 2]], axis=1)
        return (values * turn_ref[0] + swapped * turn_ref[1]).astype(jnp.bfloat16)

    repeat = lambda values: jnp.concatenate([values] * fan, axis=0)
    first = repeat(span_ref[0][:, :1])
    last = repeat(span_ref[1][:, :1])
    tiles = k_ref.shape[1] // tile
    lane = lax.broadcasted_iota(jnp.int32, (1, tile), 1)
    for head in range(KVH):
        queries = [turned(head * fan + g, query_gain_ref[...]) for g in range(fan)]
        new_key = turned(HEADS + head, key_gain_ref[...]).astype(jnp.float32)
        new_value = repeat(columns_of(HEADS + KVH + head))
        q = jnp.concatenate(queries, axis=0)
        own = jnp.concatenate(
            [jnp.sum(one.astype(jnp.float32) * new_key, axis=1, keepdims=True) for one in queries], axis=0
        )
        peak = own
        loads[2 * head].wait()
        for index in range(tiles):
            keys = k_ref[head, index * tile : (index + 1) * tile]
            score = lax.dot_general(q, keys, (((1,), (1,)), ((), ())), preferred_element_type=jnp.float32)
            position = lane + index * tile
            inside = (position >= first) & (position < last)
            score = jnp.where(inside, score, -1e30)
            kept[index] = score
            peak = jnp.maximum(peak, jnp.max(score, axis=1, keepdims=True))
        own_raised = jnp.exp((own - peak) * scale)
        total = own_raised
        mixed = own_raised * new_value
        loads[2 * head + 1].wait()
        for index in range(tiles):
            raised = jnp.exp((kept[index] - peak) * scale)
            total = total + jnp.sum(raised, axis=1, keepdims=True)
            mixed = mixed + jnp.dot(
                raised.astype(jnp.bfloat16),
                v_ref[head, index * tile : (index + 1) * tile],
                preferred_element_type=jnp.float32,
            )
        result = (mixed / total).astype(out_ref.dtype)
        for g in range(fan):
            start = (head * fan + g) * width
            out_ref[start // per_out, :, start % per_out : start % per_out + width] = result[g * rows : (g + 1) * rows]


def attend(n, merged, turns, spans, query_gain, key_gain, key_cache, value_cache):
    rows = merged.shape[1]
    pool = key_cache.shape[1]
    tile = math.gcd(pool, 1024)
    return pl.pallas_call(
        functools.partial(attend_kernel, tile),
        out_shape=jax.ShapeDtypeStruct((n, rows, HEADS * HD // n), jnp.bfloat16),
        in_specs=[VMEM] * 5 + [ANY] * 2,
        out_specs=VMEM,
        scratch_shapes=[
            pltpu.VMEM((KVH, pool, HD), jnp.bfloat16),
            pltpu.VMEM((KVH, pool, HD), jnp.bfloat16),
            pltpu.VMEM((pool // tile, rows * HEADS // KVH, tile), jnp.float32),
            pltpu.SemaphoreType.DMA((KVH,)),
            pltpu.SemaphoreType.DMA((KVH,)),
        ],
        name="attend",
    )(merged, turns, spans, query_gain[None, :], key_gain[None, :], key_cache, value_cache)


def others(n):
    me = lax.axis_index("dev")
    return [lax.rem(me + step, n) for step in range(1, n)]


def tail_kernel(
    n, s, experts, a_ref, hidden_ref, gain_ref, coded_ref, w_hbm, up_hbm, down_hbm, out_ref,
    w_ref, up_ref, down_ref, load_sem, held, here, there, residual, x_ref, every, units, parts, near,
    sum_send, sum_recv, move_send, move_recv, ring_send, ring_recv, pair_send, pair_recv,
    near_send, near_recv, home_send, home_recv, back_here, back_there,
):
    me = lax.axis_index("dev")
    at = place_of(me, n)
    sub = lax.axis_index("sub")
    rows = a_ref.shape[1]
    half_rows = rows // 2
    width = hidden_ref.shape[1]
    loads = []
    for index, (source, target) in enumerate(((w_hbm, w_ref), (up_hbm.at[0], up_ref), (down_hbm.at[0], down_ref))):
        copy = pltpu.make_async_copy(source, target, load_sem.at[index])
        copy.start()
        loads.append(copy)
    partners = [lax.rem(sub + step, s) for step in range(1, s)]
    greet(others(n), partners)
    meet(n - 1 + s - 1)

    moves = {}
    order = [n // 2]
    for away in range(n // 2 - 1, 0, -1):
        order += [away, n - away]
    for lane in order:
        copy = pltpu.make_async_remote_copy(
            src_ref=a_ref.at[dev_at(at - lane, n)],
            dst_ref=held.at[lane],
            send_sem=move_send.at[lane],
            recv_sem=move_recv.at[lane],
            device_id={"dev": dev_at(at - lane, n)},
            device_id_type=MESH,
        )
        copy.start()
        moves[lane] = copy
    loads[0].wait()

    def projected(away, devs):
        lanes = (away,) if away == 0 or 2 * away == n else (away, n - away)
        if away == 0:
            features = a_ref[me]
        else:
            for lane in lanes:
                moves[lane].wait_recv()
            features = jnp.concatenate([held[lane] for lane in lanes], axis=0)
        product = jnp.dot(features, w_ref[...], preferred_element_type=jnp.float32)
        return (product[:rows], product[-rows:])

    def normed(half, total):
        chosen = pl.ds(half * half_rows, half_rows)
        value = hidden_ref[chosen, :].astype(jnp.float32) + total
        residual[chosen, :] = value
        x_ref[chosen, :width] = norm_scale(value, gain_ref[...]).astype(x_ref.dtype)
        x_ref[chosen, width:] = coded_ref[chosen, :]

    sent = ring_reduce(n, projected, half_rows, here, there, sum_send, sum_recv, normed)
    for copy in moves.values():
        copy.wait_send()

    pairs = {}

    def share(src, origin, key, half):
        for step, partner in enumerate(partners):
            copy = pltpu.make_async_remote_copy(
                src_ref=src,
                dst_ref=every.at[origin, sub, pl.ds(half * half_rows, half_rows)],
                send_sem=pair_send.at[step, origin, half],
                recv_sem=pair_recv.at[step, origin, half],
                device_id={"sub": partner},
                device_id_type=MESH,
            )
            copy.start()
            sent.append(copy)

    slot = lambda dev, half: every.at[dev, sub, pl.ds(half * half_rows, half_rows)]
    number = me * s + sub
    inner = down_ref.shape[0]
    tile = math.gcd(inner, 256)
    block = s * rows

    def expert(hop, devs):
        if hop == 0:
            for half in range(2):
                share(x_ref.at[pl.ds(half * half_rows, half_rows)], me, None, half)
            every[me, sub] = x_ref[...]
            for copy in loads[1:]:
                copy.wait()
        for dev in devs:
            for half in range(2):
                for step, partner in enumerate(partners):
                    came = every.at[dev, lax.rem(sub + s - step - 1, s), pl.ds(half * half_rows, half_rows)]
                    pltpu.make_async_remote_copy(
                        src_ref=came,
                        dst_ref=came,
                        send_sem=pair_send.at[step, dev, half],
                        recv_sem=pair_recv.at[step, dev, half],
                        device_id={"sub": partner},
                        device_id_type=MESH,
                    ).wait_recv()
        count = block * len(devs)
        whole = jnp.concatenate([every[dev].reshape(block, every.shape[3]) for dev in devs], axis=0)
        inputs = whole[:, :width]
        codes = whole[:, width:].astype(jnp.float32)
        lane = lax.broadcasted_iota(jnp.int32, codes.shape, 1)
        high = jnp.where(lane < experts, 32.0, jnp.where(lane < 2 * experts, 1.0, 0.0))
        worth = codes * high
        total = jnp.sum(worth, axis=1, keepdims=True)
        mine = jnp.where((lane == number) | (lane == number + experts), worth, 0.0)
        mine = jnp.sum(mine, axis=1, keepdims=True)
        weight = mine / total
        for start in range(0, inner, tile):
            gate = jnp.dot(inputs, up_ref[:, start : start + tile], preferred_element_type=jnp.float32)
            up = jnp.dot(inputs, up_ref[:, inner + start : inner + start + tile], preferred_element_type=jnp.float32)
            units[:count, start : start + tile] = (gate / (1.0 + jnp.exp(-gate)) * up).astype(units.dtype)
        result = jnp.dot(units[:count, :], down_ref[...], preferred_element_type=jnp.float32)
        result = result.astype(jnp.bfloat16).astype(jnp.float32)
        result = jnp.where(mine > 0.0, result * weight, 0.0).astype(parts.dtype)
        for index, dev in enumerate(devs):
            parts[dev] = result[index * block : (index + 1) * block].reshape(s, rows, width)
        for dev in devs:
            for step, partner in enumerate(partners):
                copy = pltpu.make_async_remote_copy(
                    src_ref=parts.at[dev, partner],
                    dst_ref=near.at[step, dev],
                    send_sem=near_send.at[step, dev],
                    recv_sem=near_recv.at[step, dev],
                    device_id={"sub": partner},
                    device_id_type=MESH,
                )
                copy.start()
                sent.append(copy)

    sent += ring_gather(
        n, x_ref, slot, ring_send, ring_recv, expert, lambda dev, half: share(slot(dev, half), dev, None, half)
    )

    def one(dev):
        value = parts[dev, sub].astype(jnp.float32)
        for step, partner in enumerate(partners):
            pltpu.make_async_remote_copy(
                src_ref=near.at[step, dev],
                dst_ref=near.at[step, dev],
                send_sem=near_send.at[step, dev],
                recv_sem=near_recv.at[step, dev],
                device_id={"sub": partner},
                device_id_type=MESH,
            ).wait_recv()
            value = value + near[step, dev].astype(jnp.float32)
        return value

    def routed(away, devs):
        front = one(devs[0])
        if away == 0 or 2 * away == n:
            return (front, front)
        return (front, one(devs[1]))

    def finish(half, total):
        chosen = pl.ds(half * half_rows, half_rows)
        out_ref[chosen, :] = (residual[chosen, :] + total).astype(out_ref.dtype)

    sent += ring_reduce(n, routed, half_rows, back_here, back_there, home_send, home_recv, finish)
    for copy in sent:
        copy.wait_send()


def tail(n, s, experts, a, hidden, gain, coded, w, up, down, collective_id):
    rows, width = hidden.shape
    extra = coded.shape[1]
    ring = pltpu.SemaphoreType.DMA((2, 2, n // 2))
    lanes = pltpu.SemaphoreType.DMA((n,))
    pair = pltpu.SemaphoreType.DMA((max(s - 1, 1), n, 2))
    near = pltpu.SemaphoreType.DMA((max(s - 1, 1), n))
    sums = pltpu.VMEM((2, 2, n // 2, rows // 2, width), jnp.bfloat16)
    return pl.pallas_call(
        functools.partial(tail_kernel, n, s, experts),
        out_shape=jax.ShapeDtypeStruct((rows, width), jnp.bfloat16),
        in_specs=[VMEM] * 4 + [ANY] * 3,
        out_specs=VMEM,
        scratch_shapes=[
            pltpu.VMEM(w.shape, w.dtype),
            pltpu.VMEM(up.shape[1:], up.dtype),
            pltpu.VMEM(down.shape[1:], down.dtype),
            pltpu.SemaphoreType.DMA((3,)),
            pltpu.VMEM((n,) + a.shape[1:], a.dtype),
            sums,
            sums,
            pltpu.VMEM((rows, width), jnp.float32),
            pltpu.VMEM((rows, width + extra), jnp.bfloat16),
            pltpu.VMEM((n, s, rows, width + extra), jnp.bfloat16),
            pltpu.VMEM((2 * s * rows, down.shape[1]), jnp.bfloat16),
            pltpu.VMEM((n, s, rows, width), jnp.bfloat16),
            pltpu.VMEM((max(s - 1, 1), n, rows, width), jnp.bfloat16),
            ring, ring, lanes, lanes, ring, ring, pair, pair, near, near, ring, ring, sums, sums,
        ],
        compiler_params=pltpu.CompilerParams(collective_id=collective_id, has_side_effects=True),
        name="tail",
    )(a, hidden, gain[None, :], coded, w, up, down)


def on_device(
    n,
    s,
    hidden,
    lengths,
    key_cache,
    value_cache,
    expert_ids,
    gate_codes,
    expert_device,
    attention_gain,
    mixture_gain,
    query_gain,
    key_gain,
    project_weight,
    output_weight,
    expert_gate_up,
    expert_down,
):
    merged, turns, spans, coded = project(
        n, hidden, attention_gain, lengths, expert_ids, gate_codes, expert_device, project_weight, 0
    )
    attention = attend(n, merged, turns, spans, query_gain, key_gain, key_cache, value_cache)
    experts = expert_device.shape[0]
    return tail(
        n, s, experts, attention, hidden, mixture_gain, coded, output_weight, expert_gate_up, expert_down, 1
    )


def solution(mesh):
    return jax.shard_map(
        functools.partial(on_device, mesh.shape["dev"], mesh.shape["sub"]),
        mesh=mesh,
        in_specs=(
            P(("groups", "dev", "sub"), None),
            P(("groups", "dev", "sub"), None),
            P(("groups", "dev", "sub"), None, None),
            P(("groups", "dev", "sub"), None, None),
            P(("groups", "dev", "sub"), None),
            P(("groups", "dev", "sub"), None),
            P(),
            P(),
            P(),
            P(),
            P(),
            P(None, "dev"),
            P("dev", None),
            P(("dev", "sub"), None, None),
            P(("dev", "sub"), None, None),
        ),
        out_specs=P(("groups", "dev", "sub"), None),
        check_vma=False,
    )
```

time: 154 us -> 111 us (0.72)
  other arithmetic: 21.9 us -> 0 us
  matrix products: 9.4 us -> 0 us
  local copies, waits for them, and re-layouts: 11.3 us -> 4.29 us
  Pallas kernels: 110 us -> 107 us
    dot_general x2 -> x0, matrix products: 9.4 us -> none  [the longest x1 6.17 us: on_device(): jnp.dot(arrived, expert_gate_up[0], preferred_element_type=jnp.float32)]
    convert_element_type x5 -> x0, other arithmetic: 6.22 us -> none  [the longest x1 1.66 us: on_device(): norm_scale(hidden.astype(jnp.float32), attention_gain).astype(jnp.bfloat16)]
    reduce_sum x6 -> x0, other arithmetic: 5.14 us -> none  [the longest x4 3.89 us: norm_scale(): mean_square = jnp.mean(values * values, axis=-1, keepdims=True)]
    another operation x5 -> x0, local copies, waits for them, and re-layouts: 4.78 us -> none  [the longest x2 2.57 us: on_device(): attention.reshape(rows, n, depth).transpose(1, 0, 2)]
    unnamed x15 -> x3, local copies, waits for them, and re-layouts: 0.12 us -> 4.29 us
    pallas_call x5 -> x3, Pallas kernels: 110 us -> 107 us  [the longest x1 62 us: tail(): pl.pallas_call(functools.partial(tail_kernel, n, s, experts), out_shape=j...]
    reshape x3 -> x0, local copies, waits for them, and re-layouts: 3.08 us -> none  [the longest x1 1.47 us: on_device(): new_keys = merged[:, split:new].astype(jnp.float32).reshape(rows, KVH, HD)]
    eq x3 -> x0, other arithmetic: 2.03 us -> none  [the longest x1 0.74 us: on_device(): at_slot = (expert_device[:, None] == numbers[None, :])[None, None]]
where the time goes in v2:
time: 111 us
  Pallas kernels  107 us (96%)
  local copies, waits for them, and re-layouts  4.29 us (4%)
    pallas_call x1, Pallas kernels, tail(): pl.pallas_call(functools.partial(tail_kernel, n, s, experts), out_shape=j...  62 us
    pallas_call x1, Pallas kernels, project(): pl.pallas_call(functools.partial(project_kernel, n), out_shape=(jax.Shape...  31.2 us
    pallas_call x1, Pallas kernels, attend(): pl.pallas_call(functools.partial(attend_kernel, tile), out_shape=jax.Shap...  13.5 us
    unnamed x3, local copies, waits for them, and re-layouts  4.29 us

profile of v2, /device:TPU:0, one launch (start us, length us, event | category | flops | bytes accessed | tf_op | source)
XLA Modules:
  0.0 111.1 jit_solution(16155393155397249450)
XLA Ops:
  0.0 1.4 %copy.17.id_ref = s32[32,8]{1,0:T(8,128)} copy(s32[32,8]{0,1:T(8,128)} %param.20) | data formatting | bytes 2048 | tf_op args[4]
  1.4 1.4 %copy.18.code_ref = s32[32,8]{1,0:T(8,128)} copy(s32[32,8]{0,1:T(8,128)} %param.21) | data formatting | bytes 2048 | tf_op args[5]
  2.7 31.2 %project.1 = (bf16[8,32,640]{2,1,0:T(8,128)(2,1)}, f32[2,32,128]{2,1,0:T(8,128)}, s32[2,32,128]{2,1,0:T(8,128)}, bf16[32,128]{1,0:T(8,128)(2,1)}) custom-call(bf16[32,2048]{1,0:T(8,128)(2,1)} %hidden_ref.3, f32[1,2048]{1,0:T(1,128)} %bitcast.5, f32[1,128]{1,0:T(1,128)} %constant.2.clone.rate_ref, s32[1,32]{1,0:T(1,128)} %length_ref.1, s32[32,8]{1,0:T(8,128)} %copy.17.id_ref, ...), custom_call_target="tpu_custom_call" | custom-call | tf_op jit(solution)/shard_map/project/pallas_call | solution.py:249
  34.0 13.5 %attend.1.a_ref = bf16[8,32,512]{2,1,0:T(8,128)(2,1)} custom-call(bf16[8,32,640]{2,1,0:T(8,128)(2,1)} %get-tuple-element.9.merged_ref, f32[2,32,128]{2,1,0:T(8,128)} %get-tuple-element.10.turn_ref, s32[2,32,128]{2,1,0:T(8,128)} %get-tuple-element.11.span_ref, f32[1,128]{1,0:T(1,128)} %bitcast.7, f32[1,128]{1,0:T(1,128)} %bitcast.8, ...), custom_call_target="tpu_custom_call" | custom-call | tf_op jit(solution)/shard_map/attend/pallas_call | solution.py:355
  47.5 62.0 %tail.1 = bf16[32,2048]{1,0:T(8,128)(2,1)} custom-call(bf16[8,32,512]{2,1,0:T(8,128)(2,1)} %attend.1.a_ref, bf16[32,2048]{1,0:T(8,128)(2,1)} %hidden_ref.3, f32[1,2048]{1,0:T(1,128)} %bitcast.6, bf16[32,128]{1,0:T(8,128)(2,1)} %get-tuple-element.12.coded_ref, bf16[512,2048]{1,0:T(8,128)(2,1)} %w_hbm.3, bf16[1,2048,1536]{2,1,0:T(8,128)(2,1)} %up_hbm.1, ...), custom_call_target="tpu_custom_call" | custom-call | tf_op jit(solution)/shard_map/tail/pallas_call | solution.py:550
  109.5 1.6 %copy.20 = bf16[32,2048]{1,0:T(8,128)(2,1)} copy(bf16[32,2048]{1,0:T(8,128)(2,1)} %tail.1) | data formatting | bytes 262144
